TPU v7x, 256 devices: a whole 4x4x8 slice. The times are simulated.
256 devices in a mesh: loop: 16 (over y, x), dp: 16 (over z, core).
Axes of the slice: x: 4, y: 4, z: 8, core: 2. Of those that a mesh axis runs over, the one named last changes fastest.
Arguments:
- tokens: bfloat16 [3584, 8192], P('dp', 'loop'), may hold values from -8 to 8
- weight: bfloat16 [8192, 14336], P('loop', 'dp'), as said below
- rounding: float32 [8192, 14336], P('loop', 'dp'), may hold values from -6 to 6
- floor_codes: int32 [8192, 14336], P('loop', 'dp'), may hold values from -1 to 15
- scale_codes: int32 [14336], P('dp'), may hold values from 12 to 15
- zero_codes: int32 [14336], P('dp'), may hold values from 0 to 15
- block_mask: int32 [128, 224], P('loop', 'dp'), may hold values from 0 to 1, as said below
Outputs:
- refined: float32 [8192, 14336], P('loop', 'dp')
Inputs may be any that keep to these rules, and one draw needn't show every extreme that they name: weight equals scales times (floor_codes - zero_point + a fraction in [0, 1)), then is rounded to bfloat16. `block_mask`: the share of surviving blocks differs between column blocks.
All inputs are finite; a program needn't handle non-finite values.
Results may differ from a plain program's by a relative error of at most 0.019.
Values may be sent and summed in bfloat16 or wider, within the bound.
A program may use at most 128 MiB of HBM per device.

v0:
```python
import jax
import jax.numpy as jnp
from jax import lax
from jax.sharding import PartitionSpec as P

BLOCK = 64
ITERS = 2
step_rate = 20.0
reg_weight = 0.05
base_scale = 0.02


def expand(block_mask):
    row_blocks, col_blocks = block_mask.shape
    spread = jnp.broadcast_to(block_mask[:, None, :, None], (row_blocks, BLOCK, col_blocks, BLOCK))
    return spread.reshape(row_blocks * BLOCK, col_blocks * BLOCK).astype(jnp.float32)


def token_product(token_rows, scaled_err):
    return lax.dot_general(
        token_rows, scaled_err, (((0,), (0,)), ((), ())), preferred_element_type=jnp.float32
    )


def per_device(tokens, weight, rounding, floor_codes, scale_codes, zero_codes, block_mask):
    gathered = lax.all_gather(tokens, "dp", axis=0, tiled=True)
    token_count = gathered.shape[0]
    scales = base_scale * jnp.exp2(scale_codes.astype(jnp.float32) * 0.25)
    zero_point = zero_codes.astype(jnp.float32)
    kept_mask = expand(block_mask)
    floors = floor_codes.astype(jnp.float32)
    in_range = ((floor_codes >= 0) & (floor_codes <= 14)).astype(jnp.float32)
    target = weight.astype(jnp.float32)
    for iteration in range(ITERS):
        relaxed = jax.nn.sigmoid(rounding)
        levels = jnp.clip(floors + relaxed, 0.0, 15.0)
        w_delta = (kept_mask * (scales[None, :] * (levels - zero_point[None, :]) - target)).astype(
            jnp.bfloat16
        )
        partial_sum = jnp.dot(gathered, w_delta, preferred_element_type=jnp.float32)
        residual = lax.psum(partial_sum.astype(jnp.bfloat16), "loop").astype(jnp.float32)
        scaled_err = (2.0 / token_count * residual).astype(jnp.bfloat16)
        gradient = token_product(gathered, scaled_err)
        centered = 2.0 * relaxed - 1.0
        descent = gradient * scales[None, :] * in_range - reg_weight * 8.0 * centered**3
        rounding = rounding - step_rate * kept_mask * descent * relaxed * (1.0 - relaxed)
    return rounding


def solution(mesh):
    placed = (
        P("dp", "loop"),
        P("loop", "dp"),
        P("loop", "dp"),
        P("loop", "dp"),
        P("dp"),
        P("dp"),
        P("loop", "dp"),
    )
    return jax.shard_map(
        per_device, mesh=mesh, in_specs=placed, out_specs=P("loop", "dp"), check_vma=False
    )
```

profile of v0, /device:TPU:1, one launch (start us, length us, event | category | flops | bytes accessed | tf_op | source)
XLA Modules:
  0.0 364.3 jit_solution(10741293267602168995)
XLA Ops:
  6.5 0.7 all-gather.2.cloned.1.call-update
  7.3 0.0 all-reduce.3.cloned.1.call-start
  7.3 0.7 convert_element_type.50
  8.0 0.1 copy.8
  8.1 2.1 broadcast_in_dim.2
  10.2 4.4 %convert_element_type.51 = f32[512,896]{0,1:T(8,128)} reshape(f32[8,64,14,64]{1,0,3,2:T(8,128)} %broadcast_in_dim.2) | data formatting | bytes 3670016 | tf_op jit(solution)/shard_map/convert_element_type | solution.py:16
  14.6 1.8 copy.9
  16.4 0.0 copy-start.1
  16.4 2.8 copy.14
  19.2 1.3 copy.13
  20.5 34.1 %all-gather.2.cloned.1.call-done = bf16[3584,512]{1,0:T(8,128)(2,1)} async-done(((bf16[224,512]{1,0:T(8,128)(2,1)}), bf16[3584,512]{1,0:T(8,128)(2,1)}) %all-gather.2.cloned.1.call-update) | async-done | bytes 3670032 | tf_op jit(solution)/shard_map/all_gather | solution.py:26
  54.7 10.1 %fusion.4 = bf16[3584,896]{0,1:T(8,128)(2,1)} fusion(bf16[3584,512]{1,0:T(8,128)(2,1)} %all-gather.2.cloned.1.call-done, f32[512,896]{0,1:T(8,128)} %convert_element_type.51, bf16[512,896]{0,1:T(8,128)(2,1)} %copy.13, s32[512,896]{0,1:T(8,128)S(1)} %copy.9, f32[512,896]{0,1:T(8,128)} %copy.14, f32[896]{0:T(1024)S(1)} %convert_element_type.54, ...), kind=kOutput, calls=%fused_computation.8 | convolution fusion | flops 3297050624 | bytes 16522240 | tf_op jit(solution)/shard_map/dot_general | solution.py:40
  64.7 0.0 all-reduce.3.cloned.1.call-update
  64.8 0.2 all-reduce.5.cloned.1.call-start
  65.0 0.4 compare_and_fusion
  65.4 131.1 %all-reduce.3.cloned.1.call-done = bf16[3584,896]{0,1:T(8,128)(2,1)} async-done(((bf16[3584,896]{0,1:T(8,128)(2,1)}), bf16[3584,896]{0,1:T(8,128)(2,1)}) %all-reduce.3.cloned.1.call-update) | async-done | bytes 6422544 | tf_op jit(solution)/shard_map/psum | solution.py:41
  196.4 9.5 %fusion.15 = f32[512,896]{0,1:T(8,128)S(1)} fusion(f32[512,896]{0,1:T(8,128)} %copy.14, pred[512,896]{0,1:T(32,128)(4,1)S(1)} %compare_and_fusion, f32[512,896]{0,1:T(8,128)} %convert_element_type.51, bf16[3584,512]{1,0:T(8,128)(2,1)} %all-gather.2.cloned.1.call-done, bf16[3584,896]{0,1:T(8,128)(2,1)} %all-reduce.3.cloned.1.call-done, ...), kind=kOutput, calls=%fused_computation.23 | convolution fusion | flops 3305766912 | bytes 16059904 | tf_op jit(solution)/shard_map/dot_general | solution.py:20
  206.0 0.0 copy-start.6
  206.0 1.2 copy-done.6
  207.2 6.2 %fusion.5 = bf16[3584,896]{0,1:T(8,128)(2,1)} fusion(bf16[3584,512]{1,0:T(8,128)(2,1)S(1)} %copy-done.5, f32[512,896]{0,1:T(8,128)S(1)} %copy-done, bf16[512,896]{0,1:T(8,128)(2,1)S(1)} %copy-done.2, s32[512,896]{0,1:T(8,128)S(1)} %copy.9, f32[512,896]{0,1:T(8,128)S(1)} %fusion.15, f32[896]{0:T(1024)S(1)} %convert_element_type.54, ...), kind=kOutput, calls=%fused_computation.9 | convolution fusion | flops 3297050624 | bytes 16522240 | tf_op jit(solution)/shard_map/dot_general | solution.py:40
  213.4 0.0 all-reduce.5.cloned.1.call-update
  213.4 133.4 %all-reduce.5.cloned.1.call-done = bf16[3584,896]{0,1:T(8,128)(2,1)} async-done(((bf16[3584,896]{0,1:T(8,128)(2,1)}), bf16[3584,896]{0,1:T(8,128)(2,1)}) %all-reduce.5.cloned.1.call-update) | async-done | bytes 6422544 | tf_op jit(solution)/shard_map/psum | solution.py:41
  346.7 9.4 %fusion.21 = f32[512,896]{0,1:T(8,128)S(1)} fusion(f32[512,896]{0,1:T(8,128)} %copy-done.6, pred[512,896]{0,1:T(32,128)(4,1)S(1)} %compare_and_fusion, f32[512,896]{0,1:T(8,128)} %convert_element_type.51, bf16[3584,512]{1,0:T(8,128)(2,1)} %all-gather.2.cloned.1.call-done, bf16[3584,896]{0,1:T(8,128)(2,1)} %all-reduce.5.cloned.1.call-done, ...), kind=kOutput, calls=%fused_computation.29 | convolution fusion | flops 3305766912 | bytes 16059904 | tf_op jit(solution)/shard_map/dot_general | solution.py:20
  356.1 1.7 copy.15
  (14 shorter events, 0.0 us)
Async XLA Ops:
  6.5 48.1 %all-gather.2.cloned.1.call-start = ((), (), s32[]{:S(2)}) async-start(), calls=%async_computation | async-start | bytes 3899392 | tf_op jit(solution)/shard_map/all_gather | solution.py:26
  7.3 189.2 %all-reduce.3.cloned.1.call-start = ((), (), s32[]{:S(2)}) async-start(), calls=%async_computation.1 | async-start | bytes 12845056 | tf_op jit(solution)/shard_map/psum | solution.py:41
  16.4 2.8 copy-start.1
  16.4 4.1 %copy-start.3 = (s32[896]{0:T(1024)S(1)}, s32[896]{0:T(1024)}, u32[]{:S(2)}) copy-start(s32[896]{0:T(1024)} %param.12) | copy-start | bytes 10756
  19.2 1.3 copy-start.4
  64.8 282.0 %all-reduce.5.cloned.1.call-start = ((), (), s32[]{:S(2)}) async-start(), calls=%async_computation.2 | async-start | bytes 12845056 | tf_op jit(solution)/shard_map/psum | solution.py:41
  65.4 141.8 %copy-start.2 = (bf16[512,896]{0,1:T(8,128)(2,1)S(1)}, bf16[512,896]{0,1:T(8,128)(2,1)}, u32[]{:S(2)}) copy-start(bf16[512,896]{0,1:T(8,128)(2,1)} %copy.13) | copy-start | bytes 2752516
  196.4 10.8 %copy-start = (f32[512,896]{0,1:T(8,128)S(1)}, f32[512,896]{0,1:T(8,128)}, u32[]{:S(2)}) copy-start(f32[512,896]{0,1:T(8,128)} %convert_element_type.51) | copy-start | bytes 5505028
  196.4 10.8 %copy-start.5 = (bf16[3584,512]{1,0:T(8,128)(2,1)S(1)}, bf16[3584,512]{1,0:T(8,128)(2,1)}, u32[]{:S(2)}) copy-start(bf16[3584,512]{1,0:T(8,128)(2,1)} %all-gather.2.cloned.1.call-done) | copy-start | bytes 11010052
  206.0 1.2 copy-start.6
Sparse Core Ops, SparseCore 0:
  9.2 45.4 all-gather.1
  64.9 131.5 all-reduce.2
  213.5 133.2 all-reduce.4
where the time goes:
time: 365 us; the launch traced here: 364 us
  waiting for transfers between devices  299 us (82%)
  matrix products  35.1 us (10%)
  local copies, waits for them, and re-layouts  15.4 us (4%)
  between operations  13.2 us (4%)
    psum x2, waiting for transfers between devices, per_device(): lax.psum(partial_sum.astype(jnp.bfloat16), 'loop').astype(jnp.float32)  264 us
    all_gather x1, waiting for transfers between devices, per_device(): gathered = lax.all_gather(tokens, 'dp', axis=0, tiled=True)  34.1 us
    dot_general x2, matrix products, token_product(): lax.dot_general(token_rows, scaled_err, (((0,), (0,)), ((), ())), preferr...  18.9 us
    dot_general x2, matrix products, per_device(): partial_sum = jnp.dot(gathered, w_delta, preferred_element_type=jnp.float32)  16.2 us
  transfers between devices with their start and end apart: 3, of which 3 were waited for; matrix products, arithmetic and copies ran while one was open for 4% of the time, Pallas kernels for 0%

commit v1 on v0

--- a/solution.py
+++ b/solution.py
@@ -8,6 +8,29 @@
 step_rate = 20.0
 reg_weight = 0.05
 base_scale = 0.02
+
+
+def _detail_shapes(work_x, group_axis, dim_i):
+    later, extra, y_new = (
+        lax.axis_size(group_axis),
+        lax.axis_index(group_axis),
+        work_x.shape[dim_i],
+    )
+    steps_seen = [(i0, (i0 + 1) % later) for i0 in range(later)]
+    pool = [(i0, (i0 - 1) % later) for i0 in range(later)]
+    r1 = jnp.zeros((*work_x.shape[:dim_i], later * y_new, *work_x.shape[dim_i + 1 :]), work_x.dtype)
+    r1 = lax.dynamic_update_slice_in_dim(r1, work_x, extra * y_new, axis=dim_i)
+    clean = wide_out = work_x
+    side_arr = later // 2
+    for b in range(1, side_arr + 1):
+        clean = lax.ppermute(clean, perm=steps_seen, axis_name=group_axis)
+        r1 = lax.dynamic_update_slice_in_dim(r1, clean, (extra - b) % later * y_new, axis=dim_i)
+        if b < later - side_arr:
+            wide_out = lax.ppermute(wide_out, group_axis, perm=pool)
+            r1 = lax.dynamic_update_slice_in_dim(
+                r1, wide_out, (extra + b) % later * y_new, axis=dim_i
+            )
+    return r1
 
 
 def expand(block_mask):
@@ -23,7 +46,7 @@
 
 
 def per_device(tokens, weight, rounding, floor_codes, scale_codes, zero_codes, block_mask):
-    gathered = lax.all_gather(tokens, "dp", axis=0, tiled=True)
+    gathered = _detail_shapes(tokens, "dp", 0)
     token_count = gathered.shape[0]
     scales = base_scale * jnp.exp2(scale_codes.astype(jnp.float32) * 0.25)
     zero_point = zero_codes.astype(jnp.float32)

time: 365 us -> 383 us (1.049)
  starting transfers between devices: 0.26 us -> 34 us
  waiting for transfers between devices: 299 us -> 274 us
  local copies, waits for them, and re-layouts: 15.4 us -> 21.6 us
    all_gather x1 -> x0, waiting for transfers between devices: 34.1 us -> none  [per_device(): gathered = lax.all_gather(tokens, 'dp', axis=0, tiled=True)]
    ppermute x0 -> x15, starting transfers between devices: none -> 33.7 us  [the longest x7 32.4 us: _detail_shapes(): wide_out = lax.ppermute(wide_out, group_axis, perm=pool)]
    dynamic_update_slice x0 -> x16, local copies, waits for them, and re-layouts: none -> 11.3 us  [the longest x8 5.71 us: _detail_shapes(): lax.dynamic_update_slice_in_dim(r1, clean, (extra - b) % later * y_new, a...]
    ppermute x0 -> x15, waiting for transfers between devices: none -> 7 us  [the longest x8 6.58 us: _detail_shapes(): clean = lax.ppermute(clean, perm=steps_seen, axis_name=group_axis)]
    unnamed x17 -> x20, local copies, waits for them, and re-layouts: 7.17 us -> 1.26 us
  transfers between devices with their start and end apart: 3 -> 17, of which waited for: 3 -> 5; matrix products, arithmetic and copies ran while one was open for 4% -> 6% of each run, Pallas kernels for 0% -> 0%
where the time goes in v1:
time: 383 us
  waiting for transfers between devices  274 us (72%)
  matrix products  37.9 us (10%)
  starting transfers between devices  34 us (9%)
  local copies, waits for them, and re-layouts  21.6 us (6%)
  between operations  13.5 us (4%)
    psum x2, waiting for transfers between devices, per_device(): lax.psum(partial_sum.astype(jnp.bfloat16), 'loop').astype(jnp.float32)  267 us
    ppermute x7, starting transfers between devices, _detail_shapes(): wide_out = lax.ppermute(wide_out, group_axis, perm=pool)  32.4 us
    dot_general x2, matrix products, token_product(): lax.dot_general(token_rows, scaled_err, (((0,), (0,)), ((), ())), preferr...  20 us
    dot_general x2, matrix products, per_device(): partial_sum = jnp.dot(gathered, w_delta, preferred_element_type=jnp.float32)  17.9 us
  transfers between devices with their start and end apart: 17, of which 5 were waited for; matrix products, arithmetic and copies ran while one was open for 6% of the time, Pallas kernels for 0%

profile of v1, /device:TPU:1, one launch (start us, length us, event | category | flops | bytes accessed | tf_op | source)
XLA Modules:
  0.0 383.2 jit_solution(3855963620508707117)
XLA Ops:
  6.5 3.2 collective-permute-start.1
  9.8 2.0 broadcast_in_dim.5
  12.6 2.1 broadcast_in_dim.4
  14.7 3.1 convert_element_type.45
  17.8 1.7 copy.9
  19.5 3.6 collective-permute-start.3
  23.1 0.7 constant_dynamic-update-slice_fusion.14
  25.0 4.6 %collective-permute-start.5 = (bf16[224,512]{1,0:T(8,128)(2,1)S(1)}, bf16[224,512]{1,0:T(8,128)(2,1)S(1)}, u32[]{:S(2)}, u32[]{:S(2)}) collective-permute-start(bf16[224,512]{1,0:T(8,128)(2,1)S(1)} %collective-permute-done.3), channel_id=1, source_target_pairs={{0,15},{1,0},{2,1},{3,2},{4,3},{5,4},{6,5},{7,6},{8,7},{9,8},{10,9... | collective-permute-start | bytes 688136 | tf_op jit(solution)/shard_map/ppermute | solution.py:29
  31.0 5.2 %collective-permute-start.7 = (bf16[224,512]{1,0:T(8,128)(2,1)S(1)}, bf16[224,512]{1,0:T(8,128)(2,1)S(1)}, u32[]{:S(2)}, u32[]{:S(2)}) collective-permute-start(bf16[224,512]{1,0:T(8,128)(2,1)S(1)} %collective-permute-done.5), channel_id=1, source_target_pairs={{0,15},{1,0},{2,1},{3,2},{4,3},{5,4},{6,5},{7,6},{8,7},{9,8},{10,9... | collective-permute-start | bytes 688136 | tf_op jit(solution)/shard_map/ppermute | solution.py:29
  37.7 5.2 %collective-permute-start.9 = (bf16[224,512]{1,0:T(8,128)(2,1)S(1)}, bf16[224,512]{1,0:T(8,128)(2,1)S(1)}, u32[]{:S(2)}, u32[]{:S(2)}) collective-permute-start(bf16[224,512]{1,0:T(8,128)(2,1)S(1)} %collective-permute-done.7), channel_id=1, source_target_pairs={{0,15},{1,0},{2,1},{3,2},{4,3},{5,4},{6,5},{7,6},{8,7},{9,8},{10,9... | collective-permute-start | bytes 688136 | tf_op jit(solution)/shard_map/ppermute | solution.py:29
  42.9 0.7 constant_dynamic-update-slice_fusion.8
  44.4 5.2 %collective-permute-start.11 = (bf16[224,512]{1,0:T(8,128)(2,1)S(1)}, bf16[224,512]{1,0:T(8,128)(2,1)S(1)}, u32[]{:S(2)}, u32[]{:S(2)}) collective-permute-start(bf16[224,512]{1,0:T(8,128)(2,1)S(1)} %collective-permute-done.9), channel_id=1, source_target_pairs={{0,15},{1,0},{2,1},{3,2},{4,3},{5,4},{6,5},{7,6},{8,7},{9,8},{10,9... | collective-permute-start | bytes 688136 | tf_op jit(solution)/shard_map/ppermute | solution.py:29
  51.0 5.2 %collective-permute-start.13 = (bf16[224,512]{1,0:T(8,128)(2,1)S(1)}, bf16[224,512]{1,0:T(8,128)(2,1)S(1)}, u32[]{:S(2)}, u32[]{:S(2)}) collective-permute-start(bf16[224,512]{1,0:T(8,128)(2,1)S(1)} %collective-permute-done.11), channel_id=1, source_target_pairs={{0,15},{1,0},{2,1},{3,2},{4,3},{5,4},{6,5},{7,6},{8,7},{9,8},{10,9... | collective-permute-start | bytes 688136 | tf_op jit(solution)/shard_map/ppermute | solution.py:29
  57.7 2.7 collective-permute-done.12
  60.3 1.4 collective-permute-start.14
  63.1 3.9 %collective-permute-done.14 = bf16[224,512]{1,0:T(8,128)(2,1)S(1)} collective-permute-done((bf16[224,512]{1,0:T(8,128)(2,1)S(1)}, bf16[224,512]{1,0:T(8,128)(2,1)S(1)}, u32[]{:S(2)}, u32[]{:S(2)}) %collective-permute-start.14) | collective-permute-done | bytes 229408 | tf_op jit(solution)/shard_map/ppermute | solution.py:26
  67.7 9.0 %convolution_convert_fusion.1 = bf16[3584,896]{1,0:T(8,128)(2,1)} fusion(bf16[3584,512]{1,0:T(8,128)(2,1)} %constant_dynamic-update-slice_fusion, f32[512,896]{1,0:T(8,128)S(1)} %copy-done, bf16[512,896]{1,0:T(8,128)(2,1)S(1)} %copy-done.8, s32[512,896]{1,0:T(8,128)S(1)} %copy-done.1, f32[512,896]{1,0:T(8,128)S(1)} %copy-done.7, ...), kind=kOutput, calls=%fused_computation.3 | convolution fusion | flops 3297050624 | bytes 16522240 | tf_op jit(solution)/shard_map/dot_general | solution.py:63
  76.9 1.9 compare_and_fusion
  78.8 134.0 %all-reduce.3.cloned.1.call-done = bf16[3584,896]{1,0:T(8,128)(2,1)} async-done(((bf16[3584,896]{1,0:T(8,128)(2,1)}), bf16[3584,896]{1,0:T(8,128)(2,1)}) %all-reduce.3.cloned.1.call-update) | async-done | bytes 6422544 | tf_op jit(solution)/shard_map/psum | solution.py:64
  212.8 9.5 %fusion.13 = f32[512,896]{1,0:T(8,128)S(1)} fusion(f32[512,896]{1,0:T(8,128)} %param.9, pred[512,896]{1,0:T(32,128)(4,1)S(1)} %compare_and_fusion, f32[512,896]{1,0:T(8,128)S(1)} %copy-done, bf16[3584,512]{1,0:T(8,128)(2,1)} %constant_dynamic-update-slice_fusion, bf16[3584,896]{1,0:T(8,128)(2,1)} %all-reduce.3.cloned.1.call-done, ...), kind=kOutput, calls=%fused_computation.21 | convolution fusion | flops 3305766912 | bytes 16059904 | tf_op jit(solution)/shard_map/dot_general | solution.py:43
  222.2 1.2 copy-done.9
  223.5 9.0 %convolution_convert_fusion = bf16[3584,896]{1,0:T(8,128)(2,1)} fusion(bf16[3584,512]{1,0:T(8,128)(2,1)} %constant_dynamic-update-slice_fusion, f32[512,896]{1,0:T(8,128)S(1)} %copy-done, bf16[512,896]{1,0:T(8,128)(2,1)S(1)} %copy-done.8, s32[512,896]{1,0:T(8,128)S(1)} %copy-done.2, f32[512,896]{1,0:T(8,128)S(1)} %fusion.13, ...), kind=kOutput, calls=%fused_computation.2 | convolution fusion | flops 3297050624 | bytes 16522240 | tf_op jit(solution)/shard_map/dot_general | solution.py:63
  232.4 133.4 %all-reduce.5.cloned.1.call-done = bf16[3584,896]{1,0:T(8,128)(2,1)} async-done(((bf16[3584,896]{1,0:T(8,128)(2,1)}), bf16[3584,896]{1,0:T(8,128)(2,1)}) %all-reduce.5.cloned.1.call-update) | async-done | bytes 6422544 | tf_op jit(solution)/shard_map/psum | solution.py:64
  365.8 10.6 %fusion.19 = f32[512,896]{1,0:T(8,128)} fusion(f32[512,896]{1,0:T(8,128)} %copy-done.9, pred[512,896]{1,0:T(32,128)(4,1)S(1)} %compare_and_fusion, f32[512,896]{1,0:T(8,128)S(1)} %copy-done, bf16[3584,512]{1,0:T(8,128)(2,1)} %constant_dynamic-update-slice_fusion, bf16[3584,896]{1,0:T(8,128)(2,1)} %all-reduce.5.cloned.1.call-done, ...), kind=kOutput, calls=%fused_computation.27 | convolution fusion | flops 3305766912 | bytes 16059904 | tf_op jit(solution)/shard_map/dot_general | solution.py:43
  (61 shorter events, 10.7 us)
Async XLA Ops:
  6.5 206.2 %all-reduce.3.cloned.1.call-start = ((), (), s32[]{:S(2)}) async-start(), calls=%async_computation | async-start | bytes 12845056 | tf_op jit(solution)/shard_map/psum | solution.py:64
  6.5 13.0 %collective-permute-start.1 = (bf16[224,512]{1,0:T(8,128)(2,1)}, bf16[224,512]{1,0:T(8,128)(2,1)S(1)}, u32[]{:S(2)}, u32[]{:S(2)}) collective-permute-start(bf16[224,512]{1,0:T(8,128)(2,1)} %param.7), channel_id=1, source_target_pairs={{0,15},{1,0},{2,1},{3,2},{4,3},{5,4},{6,5},{7,6},{8,7},{9,8},{10,9... | collective-permute-start | bytes 688136 | tf_op jit(solution)/shard_map/ppermute | solution.py:29
  9.7 13.4 %collective-permute-start = (bf16[224,512]{1,0:T(8,128)(2,1)}, bf16[224,512]{1,0:T(8,128)(2,1)S(1)}, u32[]{:S(2)}, u32[]{:S(2)}) collective-permute-start(bf16[224,512]{1,0:T(8,128)(2,1)} %param.7), channel_id=1, source_target_pairs={{0,1},{1,2},{2,3},{3,4},{4,5},{5,6},{6,7},{7,8},{8,9},{9,10},{10,1... | collective-permute-start | bytes 688136 | tf_op jit(solution)/shard_map/ppermute | solution.py:26
  9.7 2.7 copy-start.4
  9.7 2.7 copy-start.5
  19.5 5.5 %collective-permute-start.3 = (bf16[224,512]{1,0:T(8,128)(2,1)S(1)}, bf16[224,512]{1,0:T(8,128)(2,1)S(1)}, u32[]{:S(2)}, u32[]{:S(2)}) collective-permute-start(bf16[224,512]{1,0:T(8,128)(2,1)S(1)} %collective-permute-done.1), channel_id=1, source_target_pairs={{0,15},{1,0},{2,1},{3,2},{4,3},{5,4},{6,5},{7,6},{8,7},{9,8},{10,9... | collective-permute-start | bytes 688136 | tf_op jit(solution)/shard_map/ppermute | solution.py:29
  23.1 6.5 %collective-permute-start.2 = (bf16[224,512]{1,0:T(8,128)(2,1)S(1)}, bf16[224,512]{1,0:T(8,128)(2,1)S(1)}, u32[]{:S(2)}, u32[]{:S(2)}) collective-permute-start(bf16[224,512]{1,0:T(8,128)(2,1)S(1)} %collective-permute-done), channel_id=1, source_target_pairs={{0,1},{1,2},{2,3},{3,4},{4,5},{5,6},{6,7},{7,8},{8,9},{9,10},{10,1... | collective-permute-start | bytes 688136 | tf_op jit(solution)/shard_map/ppermute | solution.py:26
  23.9 43.8 %copy-start.8 = (bf16[512,896]{1,0:T(8,128)(2,1)S(1)}, bf16[512,896]{1,0:T(8,128)(2,1)}, u32[]{:S(2)}) copy-start(bf16[512,896]{1,0:T(8,128)(2,1)} %param.8) | copy-start | bytes 2752516
  25.0 6.0 %collective-permute-start.5 = (bf16[224,512]{1,0:T(8,128)(2,1)S(1)}, bf16[224,512]{1,0:T(8,128)(2,1)S(1)}, u32[]{:S(2)}, u32[]{:S(2)}) collective-permute-start(bf16[224,512]{1,0:T(8,128)(2,1)S(1)} %collective-permute-done.3), channel_id=1, source_target_pairs={{0,15},{1,0},{2,1},{3,2},{4,3},{5,4},{6,5},{7,6},{8,7},{9,8},{10,9... | collective-permute-start | bytes 688136 | tf_op jit(solution)/shard_map/ppermute | solution.py:29
  29.6 6.7 %collective-permute-start.4 = (bf16[224,512]{1,0:T(8,128)(2,1)S(1)}, bf16[224,512]{1,0:T(8,128)(2,1)S(1)}, u32[]{:S(2)}, u32[]{:S(2)}) collective-permute-start(bf16[224,512]{1,0:T(8,128)(2,1)S(1)} %collective-permute-done.2), channel_id=1, source_target_pairs={{0,1},{1,2},{2,3},{3,4},{4,5},{5,6},{6,7},{7,8},{8,9},{9,10},{10,1... | collective-permute-start | bytes 688136 | tf_op jit(solution)/shard_map/ppermute | solution.py:26
  30.3 37.4 %copy-start.7 = (f32[512,896]{1,0:T(8,128)S(1)}, f32[512,896]{1,0:T(8,128)}, u32[]{:S(2)}) copy-start(f32[512,896]{1,0:T(8,128)} %param.9) | copy-start | bytes 5505028
  31.0 6.7 %collective-permute-start.7 = (bf16[224,512]{1,0:T(8,128)(2,1)S(1)}, bf16[224,512]{1,0:T(8,128)(2,1)S(1)}, u32[]{:S(2)}, u32[]{:S(2)}) collective-permute-start(bf16[224,512]{1,0:T(8,128)(2,1)S(1)} %collective-permute-done.5), channel_id=1, source_target_pairs={{0,15},{1,0},{2,1},{3,2},{4,3},{5,4},{6,5},{7,6},{8,7},{9,8},{10,9... | collective-permute-start | bytes 688136 | tf_op jit(solution)/shard_map/ppermute | solution.py:29
  36.3 6.7 %collective-permute-start.6 = (bf16[224,512]{1,0:T(8,128)(2,1)S(1)}, bf16[224,512]{1,0:T(8,128)(2,1)S(1)}, u32[]{:S(2)}, u32[]{:S(2)}) collective-permute-start(bf16[224,512]{1,0:T(8,128)(2,1)S(1)} %collective-permute-done.4), channel_id=1, source_target_pairs={{0,1},{1,2},{2,3},{3,4},{4,5},{5,6},{6,7},{7,8},{8,9},{9,10},{10,1... | collective-permute-start | bytes 688136 | tf_op jit(solution)/shard_map/ppermute | solution.py:26
  37.7 6.7 %collective-permute-start.9 = (bf16[224,512]{1,0:T(8,128)(2,1)S(1)}, bf16[224,512]{1,0:T(8,128)(2,1)S(1)}, u32[]{:S(2)}, u32[]{:S(2)}) collective-permute-start(bf16[224,512]{1,0:T(8,128)(2,1)S(1)} %collective-permute-done.7), channel_id=1, source_target_pairs={{0,15},{1,0},{2,1},{3,2},{4,3},{5,4},{6,5},{7,6},{8,7},{9,8},{10,9... | collective-permute-start | bytes 688136 | tf_op jit(solution)/shard_map/ppermute | solution.py:29
  42.9 6.7 %collective-permute-start.8 = (bf16[224,512]{1,0:T(8,128)(2,1)S(1)}, bf16[224,512]{1,0:T(8,128)(2,1)S(1)}, u32[]{:S(2)}, u32[]{:S(2)}) collective-permute-start(bf16[224,512]{1,0:T(8,128)(2,1)S(1)} %collective-permute-done.6), channel_id=1, source_target_pairs={{0,1},{1,2},{2,3},{3,4},{4,5},{5,6},{6,7},{7,8},{8,9},{9,10},{10,1... | collective-permute-start | bytes 688136 | tf_op jit(solution)/shard_map/ppermute | solution.py:26
  43.6 24.1 %copy-start = (f32[512,896]{1,0:T(8,128)S(1)}, f32[512,896]{1,0:T(8,128)}, u32[]{:S(2)}) copy-start(f32[512,896]{1,0:T(8,128)} %copy.9) | copy-start | bytes 5505028
  43.6 24.1 %copy-start.1 = (s32[512,896]{1,0:T(8,128)S(1)}, s32[512,896]{1,0:T(8,128)}, u32[]{:S(2)}) copy-start(s32[512,896]{1,0:T(8,128)} %param.10) | copy-start | bytes 5505028
  44.4 6.6 %collective-permute-start.11 = (bf16[224,512]{1,0:T(8,128)(2,1)S(1)}, bf16[224,512]{1,0:T(8,128)(2,1)S(1)}, u32[]{:S(2)}, u32[]{:S(2)}) collective-permute-start(bf16[224,512]{1,0:T(8,128)(2,1)S(1)} %collective-permute-done.9), channel_id=1, source_target_pairs={{0,15},{1,0},{2,1},{3,2},{4,3},{5,4},{6,5},{7,6},{8,7},{9,8},{10,9... | collective-permute-start | bytes 688136 | tf_op jit(solution)/shard_map/ppermute | solution.py:29
  49.6 6.7 %collective-permute-start.10 = (bf16[224,512]{1,0:T(8,128)(2,1)S(1)}, bf16[224,512]{1,0:T(8,128)(2,1)S(1)}, u32[]{:S(2)}, u32[]{:S(2)}) collective-permute-start(bf16[224,512]{1,0:T(8,128)(2,1)S(1)} %collective-permute-done.8), channel_id=1, source_target_pairs={{0,1},{1,2},{2,3},{3,4},{4,5},{5,6},{6,7},{7,8},{8,9},{9,10},{10,1... | collective-permute-start | bytes 688136 | tf_op jit(solution)/shard_map/ppermute | solution.py:26
  51.0 11.4 %collective-permute-start.13 = (bf16[224,512]{1,0:T(8,128)(2,1)S(1)}, bf16[224,512]{1,0:T(8,128)(2,1)S(1)}, u32[]{:S(2)}, u32[]{:S(2)}) collective-permute-start(bf16[224,512]{1,0:T(8,128)(2,1)S(1)} %collective-permute-done.11), channel_id=1, source_target_pairs={{0,15},{1,0},{2,1},{3,2},{4,3},{5,4},{6,5},{7,6},{8,7},{9,8},{10,9... | collective-permute-start | bytes 688136 | tf_op jit(solution)/shard_map/ppermute | solution.py:29
  56.2 4.1 %collective-permute-start.12 = (bf16[224,512]{1,0:T(8,128)(2,1)S(1)}, bf16[224,512]{1,0:T(8,128)(2,1)S(1)}, u32[]{:S(2)}, u32[]{:S(2)}) collective-permute-start(bf16[224,512]{1,0:T(8,128)(2,1)S(1)} %collective-permute-done.10), channel_id=1, source_target_pairs={{0,1},{1,2},{2,3},{3,4},{4,5},{5,6},{6,7},{7,8},{8,9},{9,10},{10,1... | collective-permute-start | bytes 688136 | tf_op jit(solution)/shard_map/ppermute | solution.py:26
  60.3 6.7 %collective-permute-start.14 = (bf16[224,512]{1,0:T(8,128)(2,1)S(1)}, bf16[224,512]{1,0:T(8,128)(2,1)S(1)}, u32[]{:S(2)}, u32[]{:S(2)}) collective-permute-start(bf16[224,512]{1,0:T(8,128)(2,1)S(1)} %collective-permute-done.12), channel_id=1, source_target_pairs={{0,1},{1,2},{2,3},{3,4},{4,5},{5,6},{6,7},{7,8},{8,9},{9,10},{10,1... | collective-permute-start | bytes 688136 | tf_op jit(solution)/shard_map/ppermute | solution.py:26
  76.7 289.1 %all-reduce.5.cloned.1.call-start = ((), (), s32[]{:S(2)}) async-start(), calls=%async_computation.1 | async-start | bytes 12845056 | tf_op jit(solution)/shard_map/psum | solution.py:64
  212.8 10.7 %copy-start.2 = (s32[512,896]{1,0:T(8,128)S(1)}, s32[512,896]{1,0:T(8,128)}, u32[]{:S(2)}) copy-start(s32[512,896]{1,0:T(8,128)} %param.10) | copy-start | bytes 5505028
  (3 other events, 5.0 us)
Sparse Core Ops, SparseCore 0:
  76.8 135.9 all-reduce.2
  232.6 133.2 all-reduce.4
